TPU v7x, 1024 devices: a whole 4x4x32 slice. The times are simulated.
1024 devices in a mesh: domain: 128 (over x, z_lo, core), band: 8 (over y, z_hi).
Axes of the slice: x: 4, y: 4, z: 32 (z_hi: 2, z_lo: 16; z = z_hi * 16 + z_lo), core: 2. Of those that a mesh axis runs over, the one named last changes fastest.
Arguments:
- wavefunctions: bfloat16 [49152, 16384], P('domain', 'band'), may hold values from -6 to 6
- rotation: bfloat16 [16384, 1024], P('band', 'domain'), may hold values from -0.1875 to 0.1875
- cell_matrices: bfloat16 [128, 512, 512], P('domain'), may hold values from -0.25 to 0.25
- cell_nodes: int32 [128, 512], P('domain'), may hold values from 0 to 511, as said below
- face_map: int32 [16384], P('domain'), may hold values from 0 to 383, as said below
Outputs:
- applied: float32 [49152, 1024], P('domain', 'band')
Inputs may be any that keep to these rules, and one draw needn't show every extreme that they name: `cell_nodes`: each cell names 512 distinct positions of its device's extended list (the 384 own nodes, then the 128 shared nodes of the next device); consecutive cells of a device share 128 positions; only the last cell of each device names shared nodes, and it names all of them. `face_map`: each device's block holds 128 distinct own nodes, all of them nodes of its first cell that no other of its cells names.
All inputs are finite; a program needn't handle non-finite values.
Results may differ from a plain program's by a relative error of at most 0.0029.
Values may be sent and summed in bfloat16 or wider, within the bound.
A program may use at most 32 MiB of HBM per device.

v0:
```python
import jax
import jax.numpy as jnp
from jax import lax
from jax.sharding import PartitionSpec as P


def shifted(value, axis, steps):
    count = lax.axis_size(axis)
    leading, last = (max(0, -steps), min(count, count - steps))
    return lax.ppermute(value, axis, [(source, source + steps) for source in range(leading, last)])


def cell_terms(source, matrices, index_list, segment_count):
    gathered = jnp.take(source, index_list, axis=0)
    products = jnp.einsum("cij,cjo->cio", matrices, gathered, preferred_element_type=jnp.float32)
    width = products.shape[2]
    return jax.ops.segment_sum(
        products.reshape(-1, width), index_list.reshape(-1), num_segments=segment_count
    )


def local(wavefunctions, rotation, cell_matrices, cell_nodes, face_map):
    partial_sum = jnp.dot(
        wavefunctions,
        lax.all_gather(rotation, "domain", axis=1, tiled=True),
        preferred_element_type=jnp.float32,
    )
    rotated = lax.psum_scatter(partial_sum, "band", scatter_dimension=1, tiled=True).astype(
        jnp.bfloat16
    )
    node_count = rotated.shape[0]
    shared_count = face_map.shape[0]
    segment_count = node_count + shared_count
    face_rows = jnp.take(rotated, face_map, axis=0)
    incoming = shifted(face_rows, "domain", -1)
    extended = jnp.concatenate([rotated, incoming], axis=0)
    accumulated = cell_terms(extended, cell_matrices, cell_nodes, segment_count)
    outgoing = accumulated[node_count:]
    returned = shifted(outgoing, "domain", 1)
    return accumulated[:node_count].at[face_map].add(returned)


def solution(mesh):
    in_specs = (
        P("domain", "band"),
        P("band", "domain"),
        P("domain", None, None),
        P("domain", None),
        P("domain"),
    )
    out_specs = P("domain", "band")
    return jax.shard_map(local, mesh=mesh, in_specs=in_specs, out_specs=out_specs, check_vma=False)
```

profile of v0, /device:TPU:2, one launch (start us, length us, event | category | flops | bytes accessed | tf_op | source)
XLA Modules:
  0.0 525.4 jit_solution(5354370408928638367)
XLA Ops:
  6.5 0.0 copy-start
  6.5 0.7 all-gather.2.cloned.1.call-update
  7.3 0.0 reduce-scatter.2.cloned.1.call-start
  7.3 247.1 %all-gather.2.cloned.1.call-done = bf16[2048,1024]{0,1:T(8,128)(2,1)} async-done(((bf16[2048,8]{0,1:T(8,128)(2,1)}), bf16[2048,1024]{0,1:T(8,128)(2,1)}) %all-gather.2.cloned.1.call-update) | async-done | bytes 4194320 | tf_op jit(solution)/shard_map/all_gather | solution.py:25
  254.4 0.0 copy-done
  254.4 5.2 fusion.7
  259.6 0.0 reduce-scatter.2.cloned.1.call-update
  259.6 0.6 copy-done.3
  260.3 0.0 copy-done.2
  260.3 223.2 %reduce-scatter.2.cloned.1.call-done = f32[384,128]{1,0:T(8,128)} async-done(((f32[384,1024]{1,0:T(8,128)}), f32[384,128]{1,0:T(8,128)}) %reduce-scatter.2.cloned.1.call-update) | async-done | bytes 196624 | tf_op jit(solution)/shard_map/reduce_scatter | solution.py:28
  483.6 0.9 convert_element_type.3
  484.5 0.7 gather_fusion
  485.2 0.1 broadcast_select_fusion
  485.3 1.9 collective-permute-start
  487.3 1.6 collective-permute-done
  488.8 1.3 gather_fusion.1
  490.2 0.0 copy-done.1
  490.2 0.4 convolution_bitcast_fusion
  490.6 0.1 copy.7
  490.8 2.3 scatter_custom_fusion
  493.1 3.1 collective-permute-start.1
  496.2 0.7 slice.12
  496.9 18.9 %collective-permute-done.1 = f32[128,128]{1,0:T(8,128)S(1)} collective-permute-done((f32[128,128]{1,0:T(8,128)S(1)}, f32[128,128]{1,0:T(8,128)S(1)}, u32[]{:S(2)}, u32[]{:S(2)}) %collective-permute-start.1) | collective-permute-done | bytes 65568 | tf_op jit(solution)/shard_map/ppermute | solution.py:10
  515.8 2.7 scatter_fusion
  (11 shorter events, 0.1 us)
Async XLA Ops:
  6.5 247.9 %copy-start = (bf16[384,2048]{1,0:T(8,128)(2,1)S(1)}, bf16[384,2048]{1,0:T(8,128)(2,1)}, u32[]{:S(2)}) copy-start(bf16[384,2048]{1,0:T(8,128)(2,1)} %param.5) | copy-start | bytes 4718596
  6.5 247.9 %all-gather.2.cloned.1.call-start = ((), (), s32[]{:S(2)}) async-start(), calls=%async_computation.1 | async-start | bytes 4227072 | tf_op jit(solution)/shard_map/all_gather | solution.py:25
  7.3 476.3 %reduce-scatter.2.cloned.1.call-start = ((), (), s32[]{:S(2)}) async-start(), calls=%async_computation.2 | async-start | bytes 1769472 | tf_op jit(solution)/shard_map/reduce_scatter | solution.py:28
  259.6 0.7 copy-start.3
  259.6 0.7 copy-start.2
  259.6 230.6 %copy-start.1 = (bf16[1,512,512]{2,1,0:T(8,128)(2,1)S(1)}, bf16[1,512,512]{2,1,0:T(8,128)(2,1)}, u32[]{:S(2)}) copy-start(bf16[1,512,512]{2,1,0:T(8,128)(2,1)} %param.7) | copy-start | bytes 1572868
  485.3 3.5 collective-permute-start
  493.1 22.7 %collective-permute-start.1 = (f32[128,128]{1,0:T(8,128)S(1)}, f32[128,128]{1,0:T(8,128)S(1)}, u32[]{:S(2)}, u32[]{:S(2)}) collective-permute-start(f32[128,128]{1,0:T(8,128)S(1)} %slice.13), channel_id=1, source_target_pairs={{0,8},{8,16},{16,24},{24,32},{32,40},{40,48},{48,56},{56,64},{64,7... | collective-permute-start | bytes 196616 | tf_op jit(solution)/shard_map/ppermute | solution.py:10
Sparse Core Ops, SparseCore 0:
  10.1 244.2 all-gather.1
  260.2 223.3 reduce-scatter.1
where the time goes:
time: 526 us; the launch traced here: 525 us
  waiting for transfers between devices  492 us (94%)
  between operations  13.5 us (3%)
  other arithmetic  6.14 us (1%)
  matrix products  5.63 us (1%)
    all_gather x1, waiting for transfers between devices, local(): lax.all_gather(rotation, 'domain', axis=1, tiled=True)  247 us
    reduce_scatter x1, waiting for transfers between devices, local(): lax.psum_scatter(partial_sum, 'band', scatter_dimension=1, tiled=True)  223 us
    ppermute x2, waiting for transfers between devices, shifted(): lax.ppermute(value, axis, [(source, source + steps) for source in range(l...  20.5 us
  transfers between devices with their start and end apart: 4, of which 4 were waited for; matrix products, arithmetic and copies ran while one was open for 0% of the time, Pallas kernels for 0%

commit v1 on v0

v1 whole, which is shorter than its diff:
```python
import functools

import jax
import jax.numpy as jnp
from jax import lax
from jax.experimental import pallas as pl
from jax.experimental.pallas import tpu as pltpu
from jax.sharding import PartitionSpec as P

MESH = pl.DeviceIdType.MESH
BF16, F32 = jnp.bfloat16, jnp.float32
XS, ZL, ZS, YS = 4, 16, 32, 4
DOMAIN = XS * ZL * 2
NT = (((1,), (1,)), ((), ()))
NN = (((1,), (0,)), ((), ()))
TN = (((0,), (0,)), ((), ()))


def dot(a, b, dims=NN):
    return lax.dot_general(a, b, dims, preferred_element_type=F32)


def two_words(value):
    high = value.astype(BF16)
    low = (value - high.astype(F32)).astype(BF16)
    return jnp.concatenate([high, low], axis=1)


def kernel(
    wf_hbm, rot_hbm, cell_hbm, nodes_ref, face_ref, out_ref,
    wf, held, cell, permuted, sent_y, came_y, sent_z, came_z, mine,
    corner_out, corner_in, face_out, face_in, back_out, back_in,
    load_sem, came, pair_came, express_sent, local_sent, x_sent, pair_sent,
    y_sent, y_came, z_sent, z_came, end_sent, end_came, token,
):
    d, b = lax.axis_index("domain"), lax.axis_index("band")
    x, z, core = d // 32, (d // 2) % ZL, d % 2
    y, zh = b // 2, b % 2
    q, r = z // 4, z % 4
    own, shared = out_ref.shape[0], face_ref.shape[1]
    cols = out_ref.shape[1]

    def along_z(step):
        far = (zh * ZL + z + step + ZS) % ZS
        return (x * 32 + (far % ZL) * 2 + core, y * 2 + far // ZL)

    def along_x(step):
        return (((x + step) % XS) * 32 + z * 2 + core, b)

    def along_y(step):
        return (d, ((y + step) % YS) * 2 + zh)

    def in_group(step):
        return (x * 32 + (q * 4 + (r + step) % 4) * 2 + core, b)

    pair = (x * 32 + z * 2 + (1 - core), b)
    across = (d, y * 2 + (1 - zh))

    def remote(source, target, send, recv, device):
        return pltpu.make_async_remote_copy(
            src_ref=source, dst_ref=target, send_sem=send, recv_sem=recv,
            device_id=device, device_id_type=MESH,
        )

    loads = [
        pltpu.make_async_copy(rot_hbm, held.at[d], load_sem.at[0]),
        pltpu.make_async_copy(wf_hbm, wf, load_sem.at[1]),
        pltpu.make_async_copy(cell_hbm, cell, load_sem.at[2]),
    ]
    for load in loads:
        load.start()

    barrier = pltpu.get_barrier_semaphore()
    greeted = [along_z(4), along_z(-4), pair]
    greeted += [f(i) for i in (1, 2, 3) for f in (in_group, along_x, along_y)]
    for device in greeted:
        pl.semaphore_signal(barrier, inc=1, device_id=device, device_id_type=MESH)
    pl.semaphore_wait(barrier, len(greeted))
    loads[0].wait()

    def slot(xx, zz):
        return held.at[(xx * ZL + zz) * 2 + core]

    def express(zz, up):
        way = 0 if up else 1
        return remote(
            slot(x, zz), slot(x, zz), express_sent.at[way, zz // 4],
            came.at[x * ZL + zz], along_z(4 if up else -4),
        )

    def local(zz, step):
        return remote(
            slot(x, zz), slot(x, zz), local_sent.at[step - 1, zz // 4],
            came.at[x * ZL + zz], in_group(step),
        )

    def over_x(zz, step):
        return remote(
            slot(x, zz), slot(x, zz), x_sent.at[step - 1, zz],
            came.at[x * ZL + zz], along_x(step),
        )

    def to_pair(xx, zz):
        index = xx * ZL + zz
        return remote(
            slot(xx, zz), slot(xx, zz), pair_sent.at[index],
            pair_came.at[index], pair,
        )

    def arrived(xx, zz):
        remote(
            slot(xx, zz), slot(xx, zz), pair_sent.at[xx * ZL + zz],
            came.at[xx * ZL + zz], pair,
        ).wait_recv()

    def spread(zz):
        for step in (1, 2, 3):
            over_x(zz, step).start()
        to_pair(x, zz).start()

    def from_group(qq):
        for step in (1, 2, 3):
            zz = qq * 4 + (r + step) % 4
            arrived(x, zz)
            spread(zz)

    def from_x(qq):
        for rr in range(4):
            for step in (1, 2, 3):
                xx = (x + step) % XS
                arrived(xx, qq * 4 + rr)
                to_pair(xx, qq * 4 + rr).start()

    pl.semaphore_signal(token, inc=1, device_id=along_z(4), device_id_type=MESH)

    @pl.when(q < 3)
    def _():
        express(z, True).start()

    @pl.when(q > 0)
    def _():
        express(z, False).start()

    for step in (1, 2, 3):
        local(z, step).start()
    spread(z)

    loads[2].wait()
    count = own + shared
    select = (
        lax.broadcasted_iota(jnp.int32, (count, count), 0) == nodes_ref[...]
    ).astype(F32).astype(BF16)
    rows = dot(select, cell[...]).astype(BF16)
    permuted[...] = dot(rows, select, NT).astype(BF16)

    @pl.when(d == 0)
    def _():
        corner_in[...] = jnp.zeros_like(corner_in)
        back_in[...] = jnp.zeros_like(back_in)

    @pl.when(d == DOMAIN - 1)
    def _():
        face_in[...] = jnp.zeros_like(face_in)

    from_group(q)

    def one_step(e, carry):
        pl.semaphore_wait(token, 1)
        pl.semaphore_signal(token, inc=1, device_id=along_z(4), device_id_type=MESH)
        low, high = q - e, q + e

        @pl.when(low >= 0)
        def _():
            zz = low * 4 + r
            arrived(x, zz)

            @pl.when(q < 3)
            def _():
                express(zz, True).start()

            for step in (1, 2, 3):
                local(zz, step).start()
            spread(zz)

        @pl.when(high <= 3)
        def _():
            zz = high * 4 + r
            arrived(x, zz)

            @pl.when(q > 0)
            def _():
                express(zz, False).start()

            for step in (1, 2, 3):
                local(zz, step).start()
            spread(zz)

        before_low, before_high = q - e + 1, q + e - 1

        @pl.when(before_low >= 0)
        def _():
            from_x(before_low)

        @pl.when(jnp.logical_and(before_high <= 3, e > 1))
        def _():
            from_x(before_high)

        @pl.when(low >= 0)
        def _():
            from_group(low)

        @pl.when(high <= 3)
        def _():
            from_group(high)

        return carry

    lax.fori_loop(1, 4, one_step, 0)
    pl.semaphore_wait(token, 1)

    @pl.when(q == 3)
    def _():
        from_x(0)

    @pl.when(q == 0)
    def _():
        from_x(3)

    loads[1].wait()

    def product(yy):
        for index in range(ZL):
            pltpu_wait = remote(
                held.at[0], held.at[0], pair_sent.at[0],
                pair_came.at[yy * ZL + index], pair,
            )
            pltpu_wait.wait_recv()
        block = held[pl.ds(yy * 32, 32)].astype(F32)
        block = block.reshape(2 * cols, block.shape[2]).astype(BF16)
        return dot(wf[...], block, NT)

    def y_copy(step, half):
        return remote(
            sent_y.at[step - 1, half], came_y.at[step - 1, half],
            y_sent.at[step - 1, half], y_came.at[step - 1, half], along_y(step),
        )

    for step in (2, 1, 3):
        part = product((y + step) % YS)
        low, high = part[:, :cols], part[:, cols:]
        sent_y[step - 1, 0] = jnp.where(zh == 0, high, low).astype(BF16)
        y_copy(step, 0).start()
        sent_y[step - 1, 1] = jnp.where(zh == 0, low, high).astype(BF16)
        y_copy(step, 1).start()
    part = product(y)
    low, high = part[:, :cols], part[:, cols:]
    other = jnp.where(zh == 0, high, low)
    mine[...] = jnp.where(zh == 0, low, high)

    for step in (1, 3, 2):
        y_copy(step, 0).wait_recv()
        other = other + came_y[step - 1, 0].astype(F32)
    sent_z[...] = other.astype(BF16)
    z_copy = remote(sent_z, came_z, z_sent, z_came, across)
    z_copy.start()

    after = (jnp.minimum(d + 1, DOMAIN - 1), b)
    before = (jnp.maximum(d - 1, 0), b)
    corner_copy = remote(corner_out, corner_in, end_sent.at[0], end_came.at[0], after)
    face_copy = remote(face_out, face_in, end_sent.at[1], end_came.at[1], before)
    back_copy = remote(back_out, back_in, end_sent.at[2], end_came.at[2], after)
    corner_out[...] = permuted[own:, own:]

    @pl.when(d < DOMAIN - 1)
    def _():
        corner_copy.start()

    total = mine[...]
    for step in (1, 3, 2):
        y_copy(step, 1).wait_recv()
        total = total + came_y[step - 1, 1].astype(F32)
    mine[...] = total
    pick = (
        lax.broadcasted_iota(jnp.int32, (own, shared), 0) == face_ref[...]
    ).astype(F32).astype(BF16)

    @pl.when(d > 0)
    def _():
        corner_copy.wait_recv()

    spread_corner = dot(pick, corner_in[...]).astype(BF16)

    z_copy.wait_recv()
    rotated = two_words(mine[...] + came_z[...].astype(F32))
    faces = dot(pick, rotated, TN).astype(BF16)
    face_out[...] = faces

    @pl.when(d > 0)
    def _():
        face_copy.start()

    back = dot(permuted[own:, :own], rotated)
    back_out[...] = two_words(back[:, :cols] + back[:, cols:])

    @pl.when(d < DOMAIN - 1)
    def _():
        back_copy.start()

    result = dot(permuted[:own, :own], rotated) + dot(spread_corner, faces)

    @pl.when(d < DOMAIN - 1)
    def _():
        face_copy.wait_recv()

    result = result + dot(permuted[:own, own:], face_in[...])

    @pl.when(d > 0)
    def _():
        back_copy.wait_recv()

    result = result + dot(pick, back_in[...])
    out_ref[...] = result[:, :cols] + result[:, cols:]

    for step in (1, 2, 3):
        for half in (0, 1):
            y_copy(step, half).wait_send()
    z_copy.wait_send()

    @pl.when(d < DOMAIN - 1)
    def _():
        corner_copy.wait_send()
        back_copy.wait_send()

    @pl.when(d > 0)
    def _():
        face_copy.wait_send()

    def sent_line(qq, carry):
        zz = qq * 4 + r

        @pl.when(jnp.logical_and(qq <= q, q < 3))
        def _():
            express(zz, True).wait_send()

        @pl.when(jnp.logical_and(qq >= q, q > 0))
        def _():
            express(zz, False).wait_send()

        for step in (1, 2, 3):
            local(zz, step).wait_send()
        return carry

    lax.fori_loop(0, 4, sent_line, 0)

    def sent_x(zz, carry):
        for step in (1, 2, 3):
            over_x(zz, step).wait_send()
        for xx in range(XS):
            to_pair(xx, zz).wait_send()
        return carry

    lax.fori_loop(0, ZL, sent_x, 0)


def local_step(wavefunctions, rotation, cell_matrices, cell_nodes, face_map):
    own, states = wavefunctions.shape
    shared = face_map.shape[0]
    count = own + shared
    cols = rotation.shape[1] * DOMAIN // 8
    dma = pltpu.SemaphoreType.DMA
    return pl.pallas_call(
        kernel,
        out_shape=jax.ShapeDtypeStruct((own, cols), F32),
        in_specs=[pl.BlockSpec(memory_space=pl.ANY)] * 3
        + [pl.BlockSpec(memory_space=pltpu.VMEM)] * 2,
        out_specs=pl.BlockSpec(memory_space=pltpu.VMEM),
        scratch_shapes=[
            pltpu.VMEM((own, states), BF16),
            pltpu.VMEM((DOMAIN, 8, states), BF16),
            pltpu.VMEM((count, count), BF16),
            pltpu.VMEM((count, count), BF16),
            pltpu.VMEM((3, 2, own, cols), BF16),
            pltpu.VMEM((3, 2, own, cols), BF16),
            pltpu.VMEM((own, cols), BF16),
            pltpu.VMEM((own, cols), BF16),
            pltpu.VMEM((own, cols), F32),
            pltpu.VMEM((shared, shared), BF16),
            pltpu.VMEM((shared, shared), BF16),
            pltpu.VMEM((shared, 2 * cols), BF16),
            pltpu.VMEM((shared, 2 * cols), BF16),
            pltpu.VMEM((shared, 2 * cols), BF16),
            pltpu.VMEM((shared, 2 * cols), BF16),
            dma((3,)),
            dma((XS * ZL,)),
            dma((XS * ZL,)),
            dma((2, 4)),
            dma((3, 4)),
            dma((3, ZL)),
            dma((XS * ZL,)),
            dma((3, 2)),
            dma((3, 2)),
            dma,
            dma,
            dma((3,)),
            dma((3,)),
            pltpu.SemaphoreType.REGULAR,
        ],
        compiler_params=pltpu.CompilerParams(collective_id=0, has_side_effects=True),
        name="rotate_and_apply",
    )(
        wavefunctions,
        rotation.T,
        cell_matrices.reshape(count, count),
        cell_nodes.reshape(1, count),
        face_map.reshape(1, shared),
    )


def solution(mesh):
    in_specs = (
        P("domain", "band"),
        P("band", "domain"),
        P("domain", None, None),
        P("domain", None),
        P("domain"),
    )
    out_specs = P("domain", "band")
    return jax.shard_map(
        local_step, mesh=mesh, in_specs=in_specs, out_specs=out_specs, check_vma=False
    )
```

time: 526 us -> 107 us (0.20)
  the two profiles are of different devices: /device:TPU:2 before, /device:TPU:4 now
where the time goes in v1:
time: 107 us
  Pallas kernels  106 us (99%)
  local copies, waits for them, and re-layouts  1.62 us (2%)
    pallas_call x1, Pallas kernels, local_step(): pl.pallas_call(kernel, out_shape=jax.ShapeDtypeStruct((own, cols), F32),...  106 us

profile of v1, /device:TPU:4, one launch (start us, length us, event | category | flops | bytes accessed | tf_op | source)
XLA Modules:
  0.0 107.2 jit_solution(12864960118175187794)
XLA Ops:
  0.0 105.6 %rotate_and_apply.1 = f32[384,128]{1,0:T(8,128)} custom-call(bf16[384,2048]{1,0:T(8,128)(2,1)} %wf_hbm.1, bf16[8,2048]{1,0:T(8,128)(2,1)} %bitcast.4, bf16[512,512]{1,0:T(8,128)(2,1)} %bitcast.3, s32[1,512]{1,0:T(1,128)} %nodes_ref.1, s32[1,128]{1,0:T(1,128)} %bitcast.5), custom_call_target="tpu_custom_call" | custom-call | tf_op jit(solution)/shard_map/rotate_and_apply/pallas_call | solution.py:371
  105.6 1.6 %copy.7 = f32[384,128]{1,0:T(8,128)} copy(f32[384,128]{1,0:T(8,128)} %rotate_and_apply.1) | data formatting | bytes 393216

commit v2 on v1

--- a/solution.py
+++ b/solution.py
@@ -20,16 +20,17 @@
     return lax.dot_general(a, b, dims, preferred_element_type=F32)
 
 
-def two_words(value):
+def two_words(value, axis):
     high = value.astype(BF16)
     low = (value - high.astype(F32)).astype(BF16)
-    return jnp.concatenate([high, low], axis=1)
+    return jnp.concatenate([high, low], axis=axis)
 
 
 def kernel(
     wf_hbm, rot_hbm, cell_hbm, nodes_ref, face_ref, out_ref,
-    wf, held, cell, permuted, sent_y, came_y, sent_z, came_z, mine,
+    wf, held, cell, permuted, sent_y, came_y, kept, sent_z, came_z, mine,
     corner_out, corner_in, face_out, face_in, back_out, back_in,
+    near_face_out, near_face_in, near_back_out, near_back_in,
     load_sem, came, pair_came, express_sent, local_sent, x_sent, pair_sent,
     y_sent, y_came, z_sent, z_came, end_sent, end_came, token,
 ):
@@ -39,6 +40,11 @@
     q, r = z // 4, z % 4
     own, shared = out_ref.shape[0], face_ref.shape[1]
     cols = out_ref.shape[1]
+    some = cols // 2
+    groups = (q, q + 1 - 2 * (q % 2), 2 - q // 2, 3 - 3 * (q // 2))
+    ends_up = jnp.logical_and(d % 32 == 31, d < DOMAIN - 1)
+    ends_down = jnp.logical_and(d % 32 == 0, d > 0)
+    line_end = jnp.logical_or(ends_up, ends_down)
 
     def along_z(step):
         far = (zh * ZL + z + step + ZS) % ZS
@@ -55,6 +61,9 @@
 
     pair = (x * 32 + z * 2 + (1 - core), b)
     across = (d, y * 2 + (1 - zh))
+    after = ((d + 1) % DOMAIN, b)
+    before = ((d + DOMAIN - 1) % DOMAIN, b)
+    near = ((d + DOMAIN + 2 * (d % 2) - 1) % DOMAIN, y * 2 + (1 - zh))
 
     def remote(source, target, send, recv, device):
         return pltpu.make_async_remote_copy(
@@ -75,7 +84,12 @@
     greeted += [f(i) for i in (1, 2, 3) for f in (in_group, along_x, along_y)]
     for device in greeted:
         pl.semaphore_signal(barrier, inc=1, device_id=device, device_id_type=MESH)
-    pl.semaphore_wait(barrier, len(greeted))
+
+    @pl.when(line_end)
+    def _():
+        pl.semaphore_signal(barrier, inc=1, device_id=near, device_id_type=MESH)
+
+    pl.semaphore_wait(barrier, len(greeted) + line_end.astype(jnp.int32))
     loads[0].wait()
 
     def slot(xx, zz):
@@ -153,6 +167,10 @@
     rows = dot(select, cell[...]).astype(BF16)
     permuted[...] = dot(rows, select, NT).astype(BF16)
 
+    pick = (
+        lax.broadcasted_iota(jnp.int32, (own, shared), 0) == face_ref[...]
+    ).astype(F32).astype(BF16)
+
     @pl.when(d == 0)
     def _():
         corner_in[...] = jnp.zeros_like(corner_in)
@@ -162,157 +180,169 @@
     def _():
         face_in[...] = jnp.zeros_like(face_in)
 
-    from_group(q)
-
-    def one_step(e, carry):
+    def pass_token():
         pl.semaphore_wait(token, 1)
         pl.semaphore_signal(token, inc=1, device_id=along_z(4), device_id_type=MESH)
-        low, high = q - e, q + e
-
-        @pl.when(low >= 0)
-        def _():
-            zz = low * 4 + r
-            arrived(x, zz)
-
-            @pl.when(q < 3)
-            def _():
-                express(zz, True).start()
-
-            for step in (1, 2, 3):
-                local(zz, step).start()
-            spread(zz)
-
-        @pl.when(high <= 3)
-        def _():
-            zz = high * 4 + r
-            arrived(x, zz)
-
-            @pl.when(q > 0)
-            def _():
-                express(zz, False).start()
-
-            for step in (1, 2, 3):
-                local(zz, step).start()
-            spread(zz)
-
-        before_low, before_high = q - e + 1, q + e - 1
-
-        @pl.when(before_low >= 0)
-        def _():
-            from_x(before_low)
-
-        @pl.when(jnp.logical_and(before_high <= 3, e > 1))
-        def _():
-            from_x(before_high)
-
-        @pl.when(low >= 0)
-        def _():
-            from_group(low)
-
-        @pl.when(high <= 3)
-        def _():
-            from_group(high)
-
-        return carry
-
-    lax.fori_loop(1, 4, one_step, 0)
+
+    def from_express(qq):
+        zz = qq * 4 + r
+        arrived(x, zz)
+
+        @pl.when(jnp.logical_and(qq < q, q < 3))
+        def _():
+            express(zz, True).start()
+
+        @pl.when(jnp.logical_and(qq > q, q > 0))
+        def _():
+            express(zz, False).start()
+
+        for step in (1, 2, 3):
+            local(zz, step).start()
+        spread(zz)
+
+    def y_copy(n, step):
+        return remote(
+            sent_y.at[step - 1, n], came_y.at[step - 1, n],
+            y_sent.at[step - 1, n], y_came.at[step - 1, n], along_y(step),
+        )
+
+    def z_copy(part):
+        rows = pl.ds(pl.multiple_of(part * some, some), some)
+        return remote(
+            sent_z.at[rows], came_z.at[rows], z_sent.at[part], z_came.at[part], across
+        )
+
+    def product(n):
+        qq = groups[n]
+        for xx in range(XS):
+            for rr in range(4):
+                index = xx * ZL + qq * 4 + rr
+                remote(
+                    held.at[0], held.at[0], pair_sent.at[index],
+                    pair_came.at[index], pair,
+                ).wait_recv()
+        pieces = [
+            held[pl.ds((((y + step) % YS) * ZL + qq * 4) * 2, 8)].astype(F32)
+            for step in range(YS)
+        ]
+        block = jnp.concatenate(pieces, axis=0)
+        block = block.reshape(YS * some, block.shape[2]).astype(BF16)
+        part = dot(block, wf[...], NT)
+        for step in (2, 1, 3):
+            sent_y[step - 1, n] = part[step * some:(step + 1) * some].astype(BF16)
+            y_copy(n, step).start()
+        kept[n] = part[:some]
+
+    def summed(n):
+        qq = groups[n]
+        total = kept[n]
+        for step in (1, 3, 2):
+            y_copy(n, step).wait_recv()
+            total = total + came_y[step - 1, n].astype(F32)
+        part = qq % 2
+        rows = pl.ds(pl.multiple_of(part * some, some), some)
+
+        @pl.when(qq // 2 == zh)
+        def _():
+            mine[rows] = total
+
+        @pl.when(qq // 2 != zh)
+        def _():
+            sent_z[rows] = total.astype(BF16)
+            z_copy(part).start()
+
+    from_group(groups[0])
+    pass_token()
+    from_express(groups[1])
+    from_express(groups[2])
+    pass_token()
+    from_group(groups[1])
+    from_x(groups[0])
+    from_express(groups[3])
+    pass_token()
+    from_group(groups[2])
+    loads[1].wait()
+    product(0)
+    from_x(groups[1])
+    from_group(groups[3])
     pl.semaphore_wait(token, 1)
-
-    @pl.when(q == 3)
-    def _():
-        from_x(0)
-
-    @pl.when(q == 0)
-    def _():
-        from_x(3)
-
-    loads[1].wait()
-
-    def product(yy):
-        for index in range(ZL):
-            pltpu_wait = remote(
-                held.at[0], held.at[0], pair_sent.at[0],
-                pair_came.at[yy * ZL + index], pair,
-            )
-            pltpu_wait.wait_recv()
-        block = held[pl.ds(yy * 32, 32)].astype(F32)
-        block = block.reshape(2 * cols, block.shape[2]).astype(BF16)
-        return dot(wf[...], block, NT)
-
-    def y_copy(step, half):
-        return remote(
-            sent_y.at[step - 1, half], came_y.at[step - 1, half],
-            y_sent.at[step - 1, half], y_came.at[step - 1, half], along_y(step),
-        )
-
-    for step in (2, 1, 3):
-        part = product((y + step) % YS)
-        low, high = part[:, :cols], part[:, cols:]
-        sent_y[step - 1, 0] = jnp.where(zh == 0, high, low).astype(BF16)
-        y_copy(step, 0).start()
-        sent_y[step - 1, 1] = jnp.where(zh == 0, low, high).astype(BF16)
-        y_copy(step, 1).start()
-    part = product(y)
-    low, high = part[:, :cols], part[:, cols:]
-    other = jnp.where(zh == 0, high, low)
-    mine[...] = jnp.where(zh == 0, low, high)
-
-    for step in (1, 3, 2):
-        y_copy(step, 0).wait_recv()
-        other = other + came_y[step - 1, 0].astype(F32)
-    sent_z[...] = other.astype(BF16)
-    z_copy = remote(sent_z, came_z, z_sent, z_came, across)
-    z_copy.start()
-
-    after = (jnp.minimum(d + 1, DOMAIN - 1), b)
-    before = (jnp.maximum(d - 1, 0), b)
+    product(1)
+    summed(0)
+    from_x(groups[2])
+    product(2)
+    summed(1)
+    from_x(groups[3])
+    product(3)
+    summed(2)
+    summed(3)
+
     corner_copy = remote(corner_out, corner_in, end_sent.at[0], end_came.at[0], after)
     face_copy = remote(face_out, face_in, end_sent.at[1], end_came.at[1], before)
     back_copy = remote(back_out, back_in, end_sent.at[2], end_came.at[2], after)
+    near_face = remote(
+        near_face_out, near_face_in, end_sent.at[3], end_came.at[3], near
+    )
+    near_back = remote(
+        near_back_out, near_back_in, end_sent.at[4], end_came.at[4], near
+    )
+
+    @pl.when(ends_down)
+    def _():
+        face_out[...] = dot(two_words(mine[...], 0), pick).astype(BF16)
+        face_copy.start()
+        near_face_out[...] = dot(sent_z[...], pick).astype(BF16)
+        near_face.start()
+
+    def back_words(words):
+        terms = dot(permuted[own:, :own], words, NT)
+        if words.shape[0] > cols:
+            terms = terms[:, :cols] + terms[:, cols:]
+        return two_words(terms, 1)
+
+    @pl.when(ends_up)
+    def _():
+        back_out[...] = back_words(two_words(mine[...], 0))
+        back_copy.start()
+        near_back_out[...] = back_words(sent_z[...])
+        near_back.start()
+
     corner_out[...] = permuted[own:, own:]
 
     @pl.when(d < DOMAIN - 1)
     def _():
         corner_copy.start()
 
-    total = mine[...]
-    for step in (1, 3, 2):
-        y_copy(step, 1).wait_recv()
-        total = total + came_y[step - 1, 1].astype(F32)
-    mine[...] = total
-    pick = (
-        lax.broadcasted_iota(jnp.int32, (own, shared), 0) == face_ref[...]
-    ).astype(F32).astype(BF16)
-
     @pl.when(d > 0)
     def _():
         corner_copy.wait_recv()
 
     spread_corner = dot(pick, corner_in[...]).astype(BF16)
 
-    z_copy.wait_recv()
-    rotated = two_words(mine[...] + came_z[...].astype(F32))
-    faces = dot(pick, rotated, TN).astype(BF16)
-    face_out[...] = faces
-
-    @pl.when(d > 0)
-    def _():
+    for part in (0, 1):
+        z_copy(part).wait_recv()
+    rotated = two_words(mine[...] + came_z[...].astype(F32), 0)
+    faces = dot(rotated, pick).astype(BF16)
+
+    sends_face = jnp.logical_and(d > 0, d % 32 != 0)
+    sends_back = d % 32 != 31
+
+    @pl.when(sends_face)
+    def _():
+        face_out[...] = faces
         face_copy.start()
 
-    back = dot(permuted[own:, :own], rotated)
-    back_out[...] = two_words(back[:, :cols] + back[:, cols:])
+    @pl.when(sends_back)
+    def _():
+        back_out[...] = back_words(rotated)
+        back_copy.start()
+
+    result = dot(permuted[:own, :own], rotated, NT) + dot(spread_corner, faces, NT)
 
     @pl.when(d < DOMAIN - 1)
     def _():
-        back_copy.start()
-
-    result = dot(permuted[:own, :own], rotated) + dot(spread_corner, faces)
-
-    @pl.when(d < DOMAIN - 1)
-    def _():
         face_copy.wait_recv()
 
-    result = result + dot(permuted[:own, own:], face_in[...])
+    result = result + dot(permuted[:own, own:], face_in[...], NT)
 
     @pl.when(d > 0)
     def _():
@@ -321,10 +351,22 @@
     result = result + dot(pick, back_in[...])
     out_ref[...] = result[:, :cols] + result[:, cols:]
 
+    @pl.when(ends_up)
+    def _():
+        near_face.wait_recv()
+        out_ref[...] += dot(permuted[:own, own:], near_face_in[...], NT)
+
+    @pl.when(ends_down)
+    def _():
+        near_back.wait_recv()
+        more = dot(pick, near_back_in[...])
+        out_ref[...] += more[:, :cols] + more[:, cols:]
+
     for step in (1, 2, 3):
-        for half in (0, 1):
-            y_copy(step, half).wait_send()
-    z_copy.wait_send()
+        for n in range(4):
+            y_copy(n, step).wait_send()
+    for part in (0, 1):
+        z_copy(part).wait_send()
 
     @pl.when(d < DOMAIN - 1)
     def _():
@@ -334,6 +376,14 @@
     @pl.when(d > 0)
     def _():
         face_copy.wait_send()
+
+    @pl.when(ends_down)
+    def _():
+        near_face.wait_send()
+
+    @pl.when(ends_up)
+    def _():
+        near_back.wait_send()
 
     def sent_line(qq, carry):
         zz = qq * 4 + r
@@ -379,15 +429,20 @@
             pltpu.VMEM((DOMAIN, 8, states), BF16),
             pltpu.VMEM((count, count), BF16),
             pltpu.VMEM((count, count), BF16),
-            pltpu.VMEM((3, 2, own, cols), BF16),
-            pltpu.VMEM((3, 2, own, cols), BF16),
-            pltpu.VMEM((own, cols), BF16),
-            pltpu.VMEM((own, cols), BF16),
-            pltpu.VMEM((own, cols), F32),
+            pltpu.VMEM((3, 4, cols // 2, own), BF16),
+            pltpu.VMEM((3, 4, cols // 2, own), BF16),
+            pltpu.VMEM((4, cols // 2, own), F32),
+            pltpu.VMEM((cols, own), BF16),
+            pltpu.VMEM((cols, own), BF16),
+            pltpu.VMEM((cols, own), F32),
             pltpu.VMEM((shared, shared), BF16),
             pltpu.VMEM((shared, shared), BF16),
+            pltpu.VMEM((2 * cols, shared), BF16),
+            pltpu.VMEM((2 * cols, shared), BF16),
             pltpu.VMEM((shared, 2 * cols), BF16),
             pltpu.VMEM((shared, 2 * cols), BF16),
+            pltpu.VMEM((cols, shared), BF16),
+            pltpu.VMEM((cols, shared), BF16),
             pltpu.VMEM((shared, 2 * cols), BF16),
             pltpu.VMEM((shared, 2 * cols), BF16),
             dma((3,)),
@@ -397,12 +452,12 @@
             dma((3, 4)),
             dma((3, ZL)),
             dma((XS * ZL,)),
-            dma((3, 2)),
-            dma((3, 2)),
-            dma,
-            dma,
-            dma((3,)),
-            dma((3,)),
+            dma((3, 4)),
+            dma((3, 4)),
+            dma((2,)),
+            dma((2,)),
+            dma((5,)),
+            dma((5,)),
             pltpu.SemaphoreType.REGULAR,
         ],
         compiler_params=pltpu.CompilerParams(collective_id=0, has_side_effects=True),

time: 107 us -> 85.6 us (0.80)
  the two profiles are of different devices: /device:TPU:4 before, /device:TPU:321 now
where the time goes in v2:
time: 85.6 us; the launch traced here: 85.4 us
  Pallas kernels  83.8 us (98%)
  local copies, waits for them, and re-layouts  1.62 us (2%)
    pallas_call x1, Pallas kernels, local_step(): pl.pallas_call(kernel, out_shape=jax.ShapeDtypeStruct((own, cols), F32),...  83.8 us

profile of v2, /device:TPU:321, one launch (start us, length us, event | category | flops | bytes accessed | tf_op | source)
XLA Modules:
  0.0 85.4 jit_solution(5042937178625556517)
XLA Ops:
  0.0 83.8 %rotate_and_apply.1 = f32[384,128]{1,0:T(8,128)} custom-call(bf16[384,2048]{1,0:T(8,128)(2,1)} %wf_hbm.1, bf16[8,2048]{1,0:T(8,128)(2,1)} %bitcast.4, bf16[512,512]{1,0:T(8,128)(2,1)} %bitcast.3, s32[1,512]{1,0:T(1,128)} %nodes_ref.1, s32[1,128]{1,0:T(1,128)} %bitcast.5), custom_call_target="tpu_custom_call" | custom-call | tf_op jit(solution)/shard_map/rotate_and_apply/pallas_call | solution.py:421
  83.8 1.6 %copy.7 = f32[384,128]{1,0:T(8,128)} copy(f32[384,128]{1,0:T(8,128)} %rotate_and_apply.1) | data formatting | bytes 393216

commit v3 on v2

--- a/solution.py
+++ b/solution.py
@@ -31,7 +31,7 @@
     wf, held, cell, permuted, sent_y, came_y, kept, sent_z, came_z, mine,
     corner_out, corner_in, face_out, face_in, back_out, back_in,
     near_face_out, near_face_in, near_back_out, near_back_in,
-    load_sem, came, pair_came, express_sent, local_sent, x_sent, pair_sent,
+    load_sem, came, x_came, pair_came, express_sent, local_sent, x_sent, pair_sent,
     y_sent, y_came, z_sent, z_came, end_sent, end_came, token,
 ):
     d, b = lax.axis_index("domain"), lax.axis_index("band")
@@ -41,6 +41,8 @@
     own, shared = out_ref.shape[0], face_ref.shape[1]
     cols = out_ref.shape[1]
     some = cols // 2
+    first = 1 + 2 * (r // 2)
+    farthest = (first, 2, 4 - first)
     groups = (q, q + 1 - 2 * (q % 2), 2 - q // 2, 3 - 3 * (q // 2))
     ends_up = jnp.logical_and(d % 32 == 31, d < DOMAIN - 1)
     ends_down = jnp.logical_and(d % 32 == 0, d > 0)
@@ -72,7 +74,9 @@
         )
 
     loads = [
-        pltpu.make_async_copy(rot_hbm, held.at[d], load_sem.at[0]),
+        pltpu.make_async_copy(
+            rot_hbm, held.at[core * (XS * ZL) + x * ZL + z], load_sem.at[0]
+        ),
         pltpu.make_async_copy(wf_hbm, wf, load_sem.at[1]),
         pltpu.make_async_copy(cell_hbm, cell, load_sem.at[2]),
     ]
@@ -93,57 +97,61 @@
     loads[0].wait()
 
     def slot(xx, zz):
-        return held.at[(xx * ZL + zz) * 2 + core]
+        return held.at[core * (XS * ZL) + xx * ZL + zz]
+
+    def four(xx, qq):
+        return held.at[pl.ds(core * (XS * ZL) + xx * ZL + qq * 4, 4)]
 
     def express(zz, up):
         way = 0 if up else 1
         return remote(
             slot(x, zz), slot(x, zz), express_sent.at[way, zz // 4],
-            came.at[x * ZL + zz], along_z(4 if up else -4),
+            came.at[zz], along_z(4 if up else -4),
         )
 
     def local(zz, step):
         return remote(
             slot(x, zz), slot(x, zz), local_sent.at[step - 1, zz // 4],
-            came.at[x * ZL + zz], in_group(step),
+            came.at[zz], in_group(step),
         )
 
     def over_x(zz, step):
         return remote(
             slot(x, zz), slot(x, zz), x_sent.at[step - 1, zz],
-            came.at[x * ZL + zz], along_x(step),
-        )
-
-    def to_pair(xx, zz):
-        index = xx * ZL + zz
-        return remote(
-            slot(xx, zz), slot(xx, zz), pair_sent.at[index],
-            pair_came.at[index], pair,
-        )
-
-    def arrived(xx, zz):
+            x_came.at[x, zz], along_x(step),
+        )
+
+    def to_pair(xx, qq):
+        return remote(
+            four(xx, qq), four(xx, qq), pair_sent.at[xx, qq],
+            pair_came.at[xx, qq], pair,
+        )
+
+    def arrived(zz):
         remote(
-            slot(xx, zz), slot(xx, zz), pair_sent.at[xx * ZL + zz],
-            came.at[xx * ZL + zz], pair,
+            slot(x, zz), slot(x, zz), pair_sent.at[0, 0], came.at[zz], pair
         ).wait_recv()
 
     def spread(zz):
-        for step in (1, 2, 3):
+        for step in (2, 1, 3):
             over_x(zz, step).start()
-        to_pair(x, zz).start()
 
     def from_group(qq):
         for step in (1, 2, 3):
             zz = qq * 4 + (r + step) % 4
-            arrived(x, zz)
+            arrived(zz)
             spread(zz)
+        to_pair(x, qq).start()
 
     def from_x(qq):
-        for rr in range(4):
-            for step in (1, 2, 3):
-                xx = (x + step) % XS
-                arrived(xx, qq * 4 + rr)
-                to_pair(xx, qq * 4 + rr).start()
+        for step in (1, 3, 2):
+            xx = (x + step) % XS
+            for rr in range(4):
+                remote(
+                    slot(xx, 0), slot(xx, 0), pair_sent.at[0, 0],
+                    x_came.at[xx, qq * 4 + rr], pair,
+                ).wait_recv()
+            to_pair(xx, qq).start()
 
     pl.semaphore_signal(token, inc=1, device_id=along_z(4), device_id_type=MESH)
 
@@ -155,21 +163,9 @@
     def _():
         express(z, False).start()
 
-    for step in (1, 2, 3):
+    for step in farthest:
         local(z, step).start()
     spread(z)
-
-    loads[2].wait()
-    count = own + shared
-    select = (
-        lax.broadcasted_iota(jnp.int32, (count, count), 0) == nodes_ref[...]
-    ).astype(F32).astype(BF16)
-    rows = dot(select, cell[...]).astype(BF16)
-    permuted[...] = dot(rows, select, NT).astype(BF16)
-
-    pick = (
-        lax.broadcasted_iota(jnp.int32, (own, shared), 0) == face_ref[...]
-    ).astype(F32).astype(BF16)
 
     @pl.when(d == 0)
     def _():
@@ -186,7 +182,7 @@
 
     def from_express(qq):
         zz = qq * 4 + r
-        arrived(x, zz)
+        arrived(zz)
 
         @pl.when(jnp.logical_and(qq < q, q < 3))
         def _():
@@ -196,7 +192,7 @@
         def _():
             express(zz, False).start()
 
-        for step in (1, 2, 3):
+        for step in farthest:
             local(zz, step).start()
         spread(zz)
 
@@ -215,18 +211,14 @@
     def product(n):
         qq = groups[n]
         for xx in range(XS):
-            for rr in range(4):
-                index = xx * ZL + qq * 4 + rr
-                remote(
-                    held.at[0], held.at[0], pair_sent.at[index],
-                    pair_came.at[index], pair,
-                ).wait_recv()
+            to_pair(xx, qq).wait_recv()
         pieces = [
-            held[pl.ds((((y + step) % YS) * ZL + qq * 4) * 2, 8)].astype(F32)
+            held[c * (XS * ZL) + ((y + step) % YS) * ZL + qq * 4 + rr].astype(F32)
             for step in range(YS)
+            for rr in range(4)
+            for c in (0, 1)
         ]
-        block = jnp.concatenate(pieces, axis=0)
-        block = block.reshape(YS * some, block.shape[2]).astype(BF16)
+        block = jnp.concatenate(pieces, axis=0).astype(BF16)
         part = dot(block, wf[...], NT)
         for step in (2, 1, 3):
             sent_y[step - 1, n] = part[step * some:(step + 1) * some].astype(BF16)
@@ -271,6 +263,19 @@
     from_x(groups[2])
     product(2)
     summed(1)
+
+    loads[2].wait()
+    count = own + shared
+    select = (
+        lax.broadcasted_iota(jnp.int32, (count, count), 0) == nodes_ref[...]
+    ).astype(F32).astype(BF16)
+    rows = dot(select, cell[...]).astype(BF16)
+    permuted[...] = dot(rows, select, NT).astype(BF16)
+
+    pick = (
+        lax.broadcasted_iota(jnp.int32, (own, shared), 0) == face_ref[...]
+    ).astype(F32).astype(BF16)
+
     from_x(groups[3])
     product(3)
     summed(2)
@@ -405,11 +410,12 @@
     def sent_x(zz, carry):
         for step in (1, 2, 3):
             over_x(zz, step).wait_send()
+        return carry
+
+    lax.fori_loop(0, ZL, sent_x, 0)
+    for qq in range(4):
         for xx in range(XS):
-            to_pair(xx, zz).wait_send()
-        return carry
-
-    lax.fori_loop(0, ZL, sent_x, 0)
+            to_pair(xx, qq).wait_send()
 
 
 def local_step(wavefunctions, rotation, cell_matrices, cell_nodes, face_map):
@@ -446,12 +452,13 @@
             pltpu.VMEM((shared, 2 * cols), BF16),
             pltpu.VMEM((shared, 2 * cols), BF16),
             dma((3,)),
-            dma((XS * ZL,)),
-            dma((XS * ZL,)),
+            dma((ZL,)),
+            dma((XS, ZL)),
+            dma((XS, 4)),
             dma((2, 4)),
             dma((3, 4)),
             dma((3, ZL)),
-            dma((XS * ZL,)),
+            dma((XS, 4)),
             dma((3, 4)),
             dma((3, 4)),
             dma((2,)),

time: 85.6 us -> 83.2 us (0.972)
  Pallas kernels: 83.8 us -> 81.4 us
    pallas_call x1, Pallas kernels: 83.8 us -> 81.4 us  [local_step(): pl.pallas_call(kernel, out_shape=jax.ShapeDtypeStruct((own, cols), F32),...]
where the time goes in v3:
time: 83.2 us; the launch traced here: 83 us
  Pallas kernels  81.4 us (98%)
  local copies, waits for them, and re-layouts  1.62 us (2%)
    pallas_call x1, Pallas kernels, local_step(): pl.pallas_call(kernel, out_shape=jax.ShapeDtypeStruct((own, cols), F32),...  81.4 us

profile of v3, /device:TPU:321, one launch (start us, length us, event | category | flops | bytes accessed | tf_op | source)
XLA Modules:
  0.0 83.0 jit_solution(137608100337689681)
XLA Ops:
  0.0 81.4 %rotate_and_apply.1 = f32[384,128]{1,0:T(8,128)} custom-call(bf16[384,2048]{1,0:T(8,128)(2,1)} %wf_hbm.1, bf16[8,2048]{1,0:T(8,128)(2,1)} %bitcast.4, bf16[512,512]{1,0:T(8,128)(2,1)} %bitcast.3, s32[1,512]{1,0:T(1,128)} %nodes_ref.1, s32[1,128]{1,0:T(1,128)} %bitcast.5), custom_call_target="tpu_custom_call" | custom-call | tf_op jit(solution)/shard_map/rotate_and_apply/pallas_call | solution.py:427
  81.4 1.6 %copy.7 = f32[384,128]{1,0:T(8,128)} copy(f32[384,128]{1,0:T(8,128)} %rotate_and_apply.1) | data formatting | bytes 393216

commit v4 on v3

--- a/solution.py
+++ b/solution.py
@@ -163,9 +163,9 @@
     def _():
         express(z, False).start()
 
+    spread(z)
     for step in farthest:
         local(z, step).start()
-    spread(z)
 
     @pl.when(d == 0)
     def _():
@@ -192,9 +192,9 @@
         def _():
             express(zz, False).start()
 
+        spread(zz)
         for step in farthest:
             local(zz, step).start()
-        spread(zz)
 
     def y_copy(n, step):
         return remote(
@@ -220,7 +220,7 @@
         ]
         block = jnp.concatenate(pieces, axis=0).astype(BF16)
         part = dot(block, wf[...], NT)
-        for step in (2, 1, 3):
+        for step in (1, 3, 2):
             sent_y[step - 1, n] = part[step * some:(step + 1) * some].astype(BF16)
             y_copy(n, step).start()
         kept[n] = part[:some]

time: 83.2 us -> 83.1 us (level)
  no operation moved by 1% of the time
where the time goes in v4:
time: 83.1 us; the launch traced here: 82.9 us
  Pallas kernels  81.3 us (98%)
  local copies, waits for them, and re-layouts  1.62 us (2%)
    pallas_call x1, Pallas kernels, local_step(): pl.pallas_call(kernel, out_shape=jax.ShapeDtypeStruct((own, cols), F32),...  81.3 us

profile of v4, /device:TPU:321, one launch (start us, length us, event | category | flops | bytes accessed | tf_op | source)
XLA Modules:
  0.0 82.9 jit_solution(16697111070015958676)
XLA Ops:
  0.0 81.3 %rotate_and_apply.1 = f32[384,128]{1,0:T(8,128)} custom-call(bf16[384,2048]{1,0:T(8,128)(2,1)} %wf_hbm.1, bf16[8,2048]{1,0:T(8,128)(2,1)} %bitcast.4, bf16[512,512]{1,0:T(8,128)(2,1)} %bitcast.3, s32[1,512]{1,0:T(1,128)} %nodes_ref.1, s32[1,128]{1,0:T(1,128)} %bitcast.5), custom_call_target="tpu_custom_call" | custom-call | tf_op jit(solution)/shard_map/rotate_and_apply/pallas_call | solution.py:427
  81.3 1.6 %copy.7 = f32[384,128]{1,0:T(8,128)} copy(f32[384,128]{1,0:T(8,128)} %rotate_and_apply.1) | data formatting | bytes 393216

commit v5 on v4

--- a/solution.py
+++ b/solution.py
@@ -263,6 +263,10 @@
     from_x(groups[2])
     product(2)
     summed(1)
+    from_x(groups[3])
+    product(3)
+    summed(2)
+    summed(3)
 
     loads[2].wait()
     count = own + shared
@@ -275,11 +279,6 @@
     pick = (
         lax.broadcasted_iota(jnp.int32, (own, shared), 0) == face_ref[...]
     ).astype(F32).astype(BF16)
-
-    from_x(groups[3])
-    product(3)
-    summed(2)
-    summed(3)
 
     corner_copy = remote(corner_out, corner_in, end_sent.at[0], end_came.at[0], after)
     face_copy = remote(face_out, face_in, end_sent.at[1], end_came.at[1], before)

time: 83.1 us -> 83.6 us (level)
  the two profiles are of different devices: /device:TPU:321 before, /device:TPU:261 now
where the time goes in v5:
time: 83.6 us; the launch traced here: 83.4 us
  Pallas kernels  81.8 us (98%)
  local copies, waits for them, and re-layouts  1.62 us (2%)
    pallas_call x1, Pallas kernels, local_step(): pl.pallas_call(kernel, out_shape=jax.ShapeDtypeStruct((own, cols), F32),...  81.8 us

profile of v5, /device:TPU:261, one launch (start us, length us, event | category | flops | bytes accessed | tf_op | source)
XLA Modules:
  0.0 83.4 jit_solution(7972799386536906406)
XLA Ops:
  0.0 81.8 %rotate_and_apply.1 = f32[384,128]{1,0:T(8,128)} custom-call(bf16[384,2048]{1,0:T(8,128)(2,1)} %wf_hbm.1, bf16[8,2048]{1,0:T(8,128)(2,1)} %bitcast.4, bf16[512,512]{1,0:T(8,128)(2,1)} %bitcast.3, s32[1,512]{1,0:T(1,128)} %nodes_ref.1, s32[1,128]{1,0:T(1,128)} %bitcast.5), custom_call_target="tpu_custom_call" | custom-call | tf_op jit(solution)/shard_map/rotate_and_apply/pallas_call | solution.py:426
  81.8 1.6 %copy.7 = f32[384,128]{1,0:T(8,128)} copy(f32[384,128]{1,0:T(8,128)} %rotate_and_apply.1) | data formatting | bytes 393216
